TPU v7x, 32 devices: a whole 2x2x4 slice. The times are simulated.
32 devices in a mesh: obj: 16 (over z, x, core), ep: 2 (over y).
Axes of the slice: x: 2, y: 2, z: 4, core: 2. Of those that a mesh axis runs over, the one named last changes fastest.
Arguments:
- light_curves: float32 [2048, 256], P('obj', 'ep'), may hold values from -40 to 40
- valid: int32 [2048, 256], P('obj', 'ep'), may hold values 0 or 1
- pixel: int32 [2048], P('obj'), may hold values from 0 to 63, never falling along the last dimension, each value on 1 to 64 neighbouring positions
- inv_sigma: float32 [2048], P('obj'), may hold values from 0.5 to 4
- modes_init: float32 [256, 16], P('ep'), may hold values from -6 to 6
- epoch_jitter: float32 [256], replicated, may hold values from 0 to 0.9
- freq_index: int32 [2048], replicated, may hold values from 4 to 511
Outputs:
- residual: float32 [2048, 256], P('obj', 'ep')
- power: float32 [2048, 2048], P(('obj', 'ep'))
Inputs may be any that keep to these rules, and one draw needn't show every extreme that they name: Pixels never decrease along the objects; each pixel holds 1 to 64 objects, and some pixel exactly 64.
All inputs are finite; a program needn't handle non-finite values. No bound on the sum of `valid` on one device may be relied on, other than what follows from the above.
Results may differ from a plain program's by a relative error of at most 0.0052.
Values may be sent and summed in bfloat16 or wider, within the bound.
A program may use at most 64 MiB of HBM per device.

v0:
```python
import math

import jax
import jax.numpy as jnp
from jax import lax
from jax.sharding import PartitionSpec as P

ITERS = 2


HUBER = 1.345
DAMP = 2.0
RIDGE = 0.05
HIGHEST = lax.Precision.HIGHEST
CONTRACT_FIRST = (((0,), (0,)), ((), ()))
CONTRACT_LAST = (((1,), (1,)), ((), ()))


def with_halo(cells, sides, width):
    for axis, dim in sides:
        count = lax.axis_size(axis)
        ends = count - 1
        head = lax.slice_in_dim(cells, 0, width, axis=dim)
        tail = lax.slice_in_dim(cells, cells.shape[dim] - width, cells.shape[dim], axis=dim)
        cells = jnp.concatenate(
            [
                lax.ppermute(tail, axis, [(i, (i + 1) % count) for i in range(ends)]),
                cells,
                lax.ppermute(head, axis, [((i + 1) % count, i) for i in range(ends)]),
            ],
            axis=dim,
        )
    return cells


def damped_solve(gram, target):
    order = target.shape[0]
    square = gram.reshape(order, order, gram.shape[1])
    level = jnp.arange(order)[:, None]
    lower = []
    for column_at in range(order):
        column = square[:, column_at, :] + DAMP * (level == column_at).astype(jnp.float32)
        if column_at > 0:
            earlier = jnp.stack(lower, axis=1)
            column = column - jnp.sum(earlier * earlier[column_at][None], axis=1)
        pivot = jnp.sqrt(column[column_at])
        column = jnp.where(level >= column_at, column / pivot[None, :], 0.0)
        lower.append(column)
    remain = target
    forward = []
    for column_at in range(order):
        value = remain[column_at] / lower[column_at][column_at]
        remain = remain - lower[column_at] * value[None, :]
        forward.append(value)
    solved = [None] * order
    for column_at in reversed(range(order)):
        value = forward[column_at]
        if column_at + 1 < order:
            later = jnp.stack(solved[column_at + 1 :])
            value = value - jnp.sum(lower[column_at][column_at + 1 :] * later, axis=0)
        solved[column_at] = value / lower[column_at][column_at]
    return jnp.stack(solved)


def spectrum_sums(weighted, weight, times, freqs):
    cycles = times[:, None] * freqs[None, :]
    angle = 2.0 * math.pi * (cycles - jnp.floor(cycles))
    basis = jnp.concatenate(
        [jnp.cos(angle), jnp.sin(angle), jnp.cos(2.0 * angle), jnp.sin(2.0 * angle)], axis=1
    ).astype(jnp.bfloat16)
    width = freqs.shape[0]
    by_weight = jnp.dot(weight, basis, preferred_element_type=jnp.float32)
    by_value = jnp.dot(weighted, basis[:, : 2 * width], preferred_element_type=jnp.float32)
    return (by_weight, by_value)


def powers(by_weight, by_value, total, level):
    width = by_value.shape[1] // 2
    cosine = by_weight[:, :width]
    sine = by_weight[:, width : 2 * width]
    cosine_two = by_weight[:, 2 * width : 3 * width]
    sine_two = by_weight[:, 3 * width :]
    mean_level = level / total
    ycos = by_value[:, :width] - mean_level * cosine
    ysin = by_value[:, width:] - mean_level * sine
    cc_term = 0.5 * (total + cosine_two) - cosine * cosine / total + RIDGE * total
    ss_term = 0.5 * (total - cosine_two) - sine * sine / total + RIDGE * total
    cs_term = 0.5 * sine_two - cosine * sine / total
    determinant = cc_term * ss_term - cs_term * cs_term
    return (
        ss_term * ycos * ycos + cc_term * ysin * ysin - 2.0 * cs_term * ycos * ysin
    ) / determinant


def full_spectra(values, weights, times, freqs):
    total = jnp.sum(weights, axis=1, keepdims=True, dtype=jnp.float32)
    level = jnp.sum(values, axis=1, keepdims=True, dtype=jnp.float32)
    count = freqs.shape[0]
    size = math.gcd(count, 512)
    blocks = []
    for begin in range(0, count, size):
        by_weight, by_value = spectrum_sums(values, weights, times, freqs[begin : begin + size])
        blocks.append(powers(by_weight, by_value, total, level))
    return jnp.concatenate(blocks, axis=1)


def robust_on(resid, mask_now, sigma_now, member_now, counts_now, combine):
    scaled = resid * sigma_now[:, None]
    squares = jnp.sum(mask_now * scaled * scaled, axis=1)
    partial_value = jnp.stack([jnp.dot(member_now, squares, precision=HIGHEST), counts_now])
    totals = combine(partial_value)
    spread = jnp.sqrt(totals[0] / jnp.maximum(totals[1], 1.0) + 1e-06)
    object_spread = jnp.dot(spread, member_now, precision=HIGHEST)
    zscore = scaled / object_spread[:, None]
    huber = HUBER / jnp.maximum(jnp.abs(zscore), HUBER)
    return mask_now * huber * (sigma_now * sigma_now)[:, None]


def per_device(light_curves, valid, pixel, inv_sigma, modes_init, epoch_jitter, freq_index):
    obj_count = lax.axis_size("obj")
    ep_count = lax.axis_size("ep")
    order = modes_init.shape[1]
    obj_rows, ep_cols = light_curves.shape
    npix = 4 * obj_count
    mask_f = valid.astype(jnp.float32)
    epochs_all = epoch_jitter.shape[0]
    freqs = (freq_index + 1).astype(jnp.float32) / (4.0 * epochs_all)
    pixel_ids = jnp.arange(npix, dtype=jnp.int32)[:, None]

    def pixel_combine(partial_value):
        across = lax.psum(partial_value, "ep")
        border = with_halo(across[None], (("obj", 0),), 1)
        return jnp.sum(border, axis=0)

    member = (pixel[None, :] == pixel_ids).astype(jnp.float32)
    count_part = jnp.dot(member, jnp.sum(mask_f, axis=1), precision=HIGHEST)

    def robust(resid):
        return robust_on(resid, mask_f, inv_sigma, member, count_part, pixel_combine)

    def residual_of(coef_t, modes_t):
        return light_curves - lax.dot_general(coef_t, modes_t, CONTRACT_FIRST, precision=HIGHEST)

    modes_t = modes_init.T
    coef_t = jnp.zeros((order, obj_rows), jnp.float32)
    for iteration in range(ITERS):
        object_weight = robust(residual_of(coef_t, modes_t))
        object_outer = (modes_t[:, None, :] * modes_t[None, :, :]).reshape(order * order, ep_cols)
        object_gram = lax.dot_general(object_outer, object_weight, CONTRACT_LAST, precision=HIGHEST)
        object_target = lax.dot_general(
            modes_t, object_weight * light_curves, CONTRACT_LAST, precision=HIGHEST
        )
        object_gram, object_target = lax.psum((object_gram, object_target), "ep")
        coef_t = damped_solve(object_gram, object_target)
        weight = robust(residual_of(coef_t, modes_t))
        outer = (coef_t[:, None, :] * coef_t[None, :, :]).reshape(order * order, obj_rows)
        gram = jnp.dot(outer, weight, precision=HIGHEST)
        target = jnp.dot(coef_t, weight * light_curves, precision=HIGHEST)
        gram, target = lax.psum((gram, target), "obj")
        modes_t = damped_solve(gram, target)
    residual = residual_of(coef_t, modes_t)
    final_weight = robust(residual)
    weighted = (final_weight * residual).astype(jnp.bfloat16)
    weight_b = final_weight.astype(jnp.bfloat16)
    share = obj_rows // ep_count
    times = jnp.arange(epochs_all, dtype=jnp.int32).astype(jnp.float32) + epoch_jitter
    stacked = (
        weighted.reshape(ep_count, share, ep_cols),
        weight_b.reshape(ep_count, share, ep_cols),
    )
    power = full_spectra(
        lax.all_to_all(stacked[0], "ep", split_axis=0, concat_axis=2, tiled=True)[0],
        lax.all_to_all(stacked[1], "ep", split_axis=0, concat_axis=2, tiled=True)[0],
        times,
        freqs,
    )[None][0]
    return (residual, power)


def solution(mesh):
    in_specs = (P("obj", "ep"), P("obj", "ep"), P("obj"), P("obj"), P("ep", None), P(), P())
    out_specs = (P("obj", "ep"), P(("obj", "ep"), None))
    return jax.shard_map(
        per_device, mesh=mesh, in_specs=in_specs, out_specs=out_specs, check_vma=False
    )
```

profile of v0, /device:TPU:0, one launch (start us, length us, event | category | flops | bytes accessed | tf_op | source)
XLA Modules:
  0.0 395.0 jit_solution(2589406136465870461)
XLA Ops:
  7.9 0.9 copy.21
  8.9 0.9 copy.34
  11.4 0.8 fusion.99
  12.2 5.9 %psum.91 = f32[2,64]{1,0:T(2,128)S(1)} all-reduce(f32[2,64]{1,0:T(2,128)S(1)} %pad_maximum_fusion.17), channel_id=1, replica_groups=mesh['obj'=16,'ep'=2] {'ep'}, use_global_device_ids=true, to_apply=%region_3.0 | all-reduce | flops 128 | bytes 1024 | tf_op jit(solution)/shard_map/psum | solution.py:131
  18.1 1.3 collective-permute-start.1
  19.4 3.0 collective-permute-start
  23.5 0.8 broadcast_multiply_fusion.3
  26.5 5.0 %psum.92 = f32[16,128]{1,0:T(8,128)S(1)} all-reduce(f32[16,128]{1,0:T(8,128)S(1)} %convolution_bitcast_fusion), channel_id=1, replica_groups=mesh['obj'=16,'ep'=2] {'ep'}, use_global_device_ids=true, to_apply=%region_4.0 | all-reduce | flops 2048 | bytes 16384 | tf_op jit(solution)/shard_map/psum | solution.py:153
  31.5 18.2 %all-reduce.5.cloned.1.call-done = f32[16,16,128]{2,0,1:T(8,128)} async-done(((f32[16,16,128]{2,0,1:T(8,128)}), f32[16,16,128]{2,0,1:T(8,128)}) %all-reduce.5.cloned.1.call-update) | async-done | bytes 131088 | tf_op jit(solution)/shard_map/psum | solution.py:153
  49.7 0.8 bitcast_add_fusion.59
  52.1 0.8 bitcast_subtract_fusion.55
  52.8 0.8 divide_select_fusion.59
  53.6 0.8 constant_dynamic-update-slice_fusion.93
  55.4 0.8 constant_dynamic-update-slice_fusion.92
  63.0 4.9 %psum.94 = f32[2,64]{1,0:T(2,128)S(1)} all-reduce(f32[2,64]{1,0:T(2,128)S(1)} %pad_maximum_fusion.16), channel_id=1, replica_groups=mesh['obj'=16,'ep'=2] {'ep'}, use_global_device_ids=true, to_apply=%region_35.36 | all-reduce | flops 128 | bytes 1024 | tf_op jit(solution)/shard_map/psum | solution.py:131
  68.0 1.3 collective-permute-start.3
  69.2 3.0 collective-permute-start.2
  74.5 34.2 %psum.95 = f32[16,128]{1,0:T(8,128)S(1)} all-reduce(f32[16,128]{1,0:T(8,128)S(1)} %fusion.84), channel_id=1, replica_groups=mesh['obj'=16,'ep'=2] {'obj'}, use_global_device_ids=true, to_apply=%region_36.37 | all-reduce | flops 2048 | bytes 16384 | tf_op jit(solution)/shard_map/psum | solution.py:159
  108.8 55.7 %all-reduce.7.cloned.1.call-done = f32[16,16,128]{2,0,1:T(8,128)} async-done(((f32[16,16,128]{2,0,1:T(8,128)}), f32[16,16,128]{2,0,1:T(8,128)}) %all-reduce.7.cloned.1.call-update) | async-done | bytes 131088 | tf_op jit(solution)/shard_map/psum | solution.py:159
  164.5 0.8 bitcast_add_fusion.44
  167.7 0.8 multiply_subtract_fusion.41
  168.6 0.8 constant_dynamic-update-slice_fusion.203
  178.0 4.9 %psum.97 = f32[2,64]{1,0:T(2,128)S(1)} all-reduce(f32[2,64]{1,0:T(2,128)S(1)} %pad_maximum_fusion.15), channel_id=1, replica_groups=mesh['obj'=16,'ep'=2] {'ep'}, use_global_device_ids=true, to_apply=%region_67.68 | all-reduce | flops 128 | bytes 1024 | tf_op jit(solution)/shard_map/psum | solution.py:131
  182.9 1.3 collective-permute-start.5
  184.2 3.0 collective-permute-start.4
  189.4 5.0 %psum.98 = f32[16,128]{1,0:T(8,128)S(1)} all-reduce(f32[16,128]{1,0:T(8,128)S(1)} %fusion.82), channel_id=1, replica_groups=mesh['obj'=16,'ep'=2] {'ep'}, use_global_device_ids=true, to_apply=%region_68.69 | all-reduce | flops 2048 | bytes 16384 | tf_op jit(solution)/shard_map/psum | solution.py:153
  194.4 20.6 %all-reduce.9.cloned.1.call-done = f32[16,16,128]{2,0,1:T(8,128)} async-done(((f32[16,16,128]{2,0,1:T(8,128)}), f32[16,16,128]{2,0,1:T(8,128)}) %all-reduce.9.cloned.1.call-update) | async-done | bytes 131088 | tf_op jit(solution)/shard_map/psum | solution.py:153
  215.0 0.8 bitcast_add_fusion.29
  218.3 0.8 multiply_subtract_fusion.27
  219.1 0.8 constant_dynamic-update-slice_fusion.313
  228.5 4.9 %psum.100 = f32[2,64]{1,0:T(2,128)S(1)} all-reduce(f32[2,64]{1,0:T(2,128)S(1)} %pad_maximum_fusion.14), channel_id=1, replica_groups=mesh['obj'=16,'ep'=2] {'ep'}, use_global_device_ids=true, to_apply=%region_99.100 | all-reduce | flops 128 | bytes 1024 | tf_op jit(solution)/shard_map/psum | solution.py:131
  233.5 1.3 collective-permute-start.7
  234.8 3.0 collective-permute-start.6
  240.0 34.4 %psum.101 = f32[16,128]{1,0:T(8,128)S(1)} all-reduce(f32[16,128]{1,0:T(8,128)S(1)} %fusion.80), channel_id=1, replica_groups=mesh['obj'=16,'ep'=2] {'obj'}, use_global_device_ids=true, to_apply=%region_100.101 | all-reduce | flops 2048 | bytes 16384 | tf_op jit(solution)/shard_map/psum | solution.py:159
  274.4 55.6 %all-reduce.11.cloned.1.call-done = f32[16,16,128]{2,0,1:T(8,128)} async-done(((f32[16,16,128]{2,0,1:T(8,128)}), f32[16,16,128]{2,0,1:T(8,128)}) %all-reduce.11.cloned.1.call-update) | async-done | bytes 131088 | tf_op jit(solution)/shard_map/psum | solution.py:159
  330.0 0.8 bitcast_add_fusion.14
  333.2 0.8 multiply_subtract_fusion.13
  334.1 0.8 constant_dynamic-update-slice_fusion.423
  343.5 4.9 %psum.103 = f32[2,64]{1,0:T(2,128)S(1)} all-reduce(f32[2,64]{1,0:T(2,128)S(1)} %pad_maximum_fusion.13), channel_id=1, replica_groups=mesh['obj'=16,'ep'=2] {'ep'}, use_global_device_ids=true, to_apply=%region_131.132 | all-reduce | flops 128 | bytes 1024 | tf_op jit(solution)/shard_map/psum | solution.py:131
  348.4 1.3 collective-permute-start.9
  349.7 3.0 collective-permute-start.8
  352.8 0.8 collective-permute-done.8
  354.5 3.3 all-to-all-start
  358.5 3.2 all-to-all-done
  361.7 3.3 all-to-all-start.1
  365.0 16.8 %cosine_convert_fusion.6 = (bf16[256,512]{1,0:T(8,128)(2,1)}, bf16[256,512]{1,0:T(8,128)(2,1)}, bf16[256,512]{1,0:T(8,128)(2,1)}, bf16[256,512]{1,0:T(8,128)(2,1...) fusion(f32[512]{0:T(512)S(1)} %get-tuple-element.130, ...), kind=kLoop, calls=%fused_computation.525 | loop fusion | flops 4718592 | bytes 4203520 | tf_op jit(solution)/shard_map/convert.14
  382.9 1.3 fusion.35
  387.7 0.8 pad_maximum_fusion
  (861 shorter events, 58.6 us)
Async XLA Ops:
  7.2 17.1 %copy-start.9 = (f32[128]{0:T(128)S(1)}, f32[128]{0:T(128)}, u32[]{:S(2)}) copy-start(f32[128]{0:T(128)} %param.10) | copy-start | bytes 1540
  7.2 17.8 %copy-start.11 = (s32[128]{0:T(128)S(1)}, s32[128]{0:T(128)}, u32[]{:S(2)}) copy-start(s32[128]{0:T(128)} %param.9) | copy-start | bytes 1540
  7.2 42.5 %all-reduce.5.cloned.1.call-start = ((), (), s32[]{:S(2)}) async-start(), calls=%async_computation.2 | async-start | bytes 262144 | tf_op jit(solution)/shard_map/psum | solution.py:153
  18.1 6.8 %collective-permute-start.1 = (f32[1,2,64]{2,1,0:T(2,128)S(1)}, f32[1,2,64]{2,1,0:T(2,128)S(1)}, u32[]{:S(2)}, u32[]{:S(2)}) collective-permute-start(f32[1,2,64]{2,1,0:T(2,128)S(1)} %bitcast.1451), channel_id=1, source_target_pairs={{2,0},{4,2},{6,4},{8,6},{10,8},{12,10},{14,12},{16,14},{18,16},{20... | collective-permute-start | bytes 1544 | tf_op jit(solution)/shard_map/ppermute | solution.py:29
  19.4 5.5 %collective-permute-start = (f32[1,2,64]{2,1,0:T(2,128)S(1)}, f32[1,2,64]{2,1,0:T(2,128)S(1)}, u32[]{:S(2)}, u32[]{:S(2)}) collective-permute-start(f32[1,2,64]{2,1,0:T(2,128)S(1)} %bitcast.1452), channel_id=1, source_target_pairs={{0,2},{2,4},{4,6},{6,8},{8,10},{10,12},{12,14},{14,16},{16,18},{18... | collective-permute-start | bytes 1544 | tf_op jit(solution)/shard_map/ppermute | solution.py:27
  24.3 1.9 copy-start.8
  26.2 138.3 %all-reduce.7.cloned.1.call-start = ((), (), s32[]{:S(2)}) async-start(), calls=%async_computation.3 | async-start | bytes 262144 | tf_op jit(solution)/shard_map/psum | solution.py:159
  49.7 6.5 %copy-start.3 = (f32[16,16,128]{2,0,1:T(8,128)S(1)}, f32[16,16,128]{2,0,1:T(8,128)}, u32[]{:S(2)}) copy-start(f32[16,16,128]{2,0,1:T(8,128)} %all-reduce.5.cloned.1.call-done) | copy-start | bytes 393220
  68.0 4.3 %collective-permute-start.3 = (f32[1,2,64]{2,1,0:T(2,128)S(1)}, f32[1,2,64]{2,1,0:T(2,128)S(1)}, u32[]{:S(2)}, u32[]{:S(2)}) collective-permute-start(f32[1,2,64]{2,1,0:T(2,128)S(1)} %bitcast.1455), channel_id=1, source_target_pairs={{2,0},{4,2},{6,4},{8,6},{10,8},{12,10},{14,12},{16,14},{18,16},{20... | collective-permute-start | bytes 1544 | tf_op jit(solution)/shard_map/ppermute | solution.py:29
  69.2 3.8 collective-permute-start.2
  74.3 140.8 %all-reduce.9.cloned.1.call-start = ((), (), s32[]{:S(2)}) async-start(), calls=%async_computation.4 | async-start | bytes 262144 | tf_op jit(solution)/shard_map/psum | solution.py:153
  164.5 6.7 %copy-start.1 = (f32[16,16,128]{2,0,1:T(8,128)S(1)}, f32[16,16,128]{2,0,1:T(8,128)}, u32[]{:S(2)}) copy-start(f32[16,16,128]{2,0,1:T(8,128)} %all-reduce.7.cloned.1.call-done) | copy-start | bytes 393220
  182.9 4.3 %collective-permute-start.5 = (f32[1,2,64]{2,1,0:T(2,128)S(1)}, f32[1,2,64]{2,1,0:T(2,128)S(1)}, u32[]{:S(2)}, u32[]{:S(2)}) collective-permute-start(f32[1,2,64]{2,1,0:T(2,128)S(1)} %bitcast.1457), channel_id=1, source_target_pairs={{2,0},{4,2},{6,4},{8,6},{10,8},{12,10},{14,12},{16,14},{18,16},{20... | collective-permute-start | bytes 1544 | tf_op jit(solution)/shard_map/ppermute | solution.py:29
  184.2 3.8 collective-permute-start.4
  189.2 140.8 %all-reduce.11.cloned.1.call-start = ((), (), s32[]{:S(2)}) async-start(), calls=%async_computation.5 | async-start | bytes 262144 | tf_op jit(solution)/shard_map/psum | solution.py:159
  215.0 6.7 %copy-start.2 = (f32[16,16,128]{2,0,1:T(8,128)S(1)}, f32[16,16,128]{2,0,1:T(8,128)}, u32[]{:S(2)}) copy-start(f32[16,16,128]{2,0,1:T(8,128)} %all-reduce.9.cloned.1.call-done) | copy-start | bytes 393220
  233.5 4.3 %collective-permute-start.7 = (f32[1,2,64]{2,1,0:T(2,128)S(1)}, f32[1,2,64]{2,1,0:T(2,128)S(1)}, u32[]{:S(2)}, u32[]{:S(2)}) collective-permute-start(f32[1,2,64]{2,1,0:T(2,128)S(1)} %bitcast.1459), channel_id=1, source_target_pairs={{2,0},{4,2},{6,4},{8,6},{10,8},{12,10},{14,12},{16,14},{18,16},{20... | collective-permute-start | bytes 1544 | tf_op jit(solution)/shard_map/ppermute | solution.py:29
  234.8 3.8 collective-permute-start.6
  330.0 6.7 %copy-start = (f32[16,16,128]{2,0,1:T(8,128)S(1)}, f32[16,16,128]{2,0,1:T(8,128)}, u32[]{:S(2)}) copy-start(f32[16,16,128]{2,0,1:T(8,128)} %all-reduce.11.cloned.1.call-done) | copy-start | bytes 393220
  341.2 16.6 %copy-start.10 = (f32[256]{0:T(256)S(1)}, f32[256]{0:T(256)}, u32[]{:S(2)}) copy-start(f32[256]{0:T(256)} %param.12) | copy-start | bytes 3076
  348.4 4.3 %collective-permute-start.9 = (f32[1,2,64]{2,1,0:T(2,128)S(1)}, f32[1,2,64]{2,1,0:T(2,128)S(1)}, u32[]{:S(2)}, u32[]{:S(2)}) collective-permute-start(f32[1,2,64]{2,1,0:T(2,128)S(1)} %bitcast.1453), channel_id=1, source_target_pairs={{2,0},{4,2},{6,4},{8,6},{10,8},{12,10},{14,12},{16,14},{18,16},{20... | collective-permute-start | bytes 1544 | tf_op jit(solution)/shard_map/ppermute | solution.py:29
  349.7 3.8 collective-permute-start.8
  354.5 7.2 %all-to-all-start = ((bf16[2,64,128]{2,1,0:T(8,128)(2,1)}), bf16[2,64,128]{2,1,0:T(8,128)(2,1)S(1)}, u32[]{:S(2)}, u32[]{:S(2)}) async-start(bf16[2,64,128]{2,1,0:T(8,128)(2,1)} %bitcast.368), calls=%async_computation | async-start | bytes 65536 | tf_op jit(solution)/shard_map/all_to_all | solution.py:173
  361.7 20.9 %all-to-all-start.1 = ((bf16[2,64,128]{2,1,0:T(8,128)(2,1)}), bf16[2,64,128]{2,1,0:T(8,128)(2,1)S(1)}, u32[]{:S(2)}, u32[]{:S(2)}) async-start(bf16[2,64,128]{2,1,0:T(8,128)(2,1)} %bitcast.372), calls=%async_computation.1 | async-start | bytes 65536 | tf_op jit(solution)/shard_map/all_to_all | solution.py:172
  382.8 1.5 copy-start.7
  384.1 1.0 copy-start.4
  384.1 1.0 copy-start.5
  384.2 1.1 copy-start.6
Sparse Core Ops, SparseCore 0:
  26.3 23.3 all-reduce.4
  74.4 90.0 all-reduce.6
  189.3 25.6 all-reduce.8
  239.9 90.0 all-reduce.10
where the time goes:
time: 402 us; the launch traced here: 395 us
  waiting for transfers between devices  156 us (39%)
  blocking collectives  104 us (26%)
  other arithmetic  68.2 us (17%)
  starting transfers between devices  28.2 us (7%)
  between operations  16.6 us (4%)
  local copies, waits for them, and re-layouts  12.2 us (3%)
  matrix products  9.14 us (2%)
    psum x2, waiting for transfers between devices, per_device(): gram, target = lax.psum((gram, target), 'obj')  111 us
    psum x2, blocking collectives, per_device(): gram, target = lax.psum((gram, target), 'obj')  68.6 us
    psum x2, waiting for transfers between devices, per_device(): object_gram, object_target = lax.psum((object_gram, object_target), 'ep')  38.8 us
    psum x5, blocking collectives, pixel_combine(): across = lax.psum(partial_value, 'ep')  25.6 us
    another operation x2, other arithmetic  17.5 us
    ppermute x5, starting transfers between devices, with_halo(): lax.ppermute(tail, axis, [(i, (i + 1) % count) for i in range(ends)])  15.2 us
    unnamed x56, other arithmetic  12.5 us
    sub x60, other arithmetic, damped_solve(): column = column - jnp.sum(earlier * earlier[column_at][None], axis=1)  10 us
  transfers between devices with their start and end apart: 16, of which 9 were waited for; matrix products, arithmetic and copies ran while one was open for 5% of the time, Pallas kernels for 0%

commit v1 on v0

v1 whole, which is shorter than its diff:
```python
import functools
import math

import jax
import jax.numpy as jnp
from jax import lax
from jax.experimental import pallas as pl
from jax.experimental.pallas import tpu as pltpu
from jax.sharding import PartitionSpec as P

ITERS = 2


HUBER = 1.345
DAMP = 2.0
RIDGE = 0.05
HIGHEST = lax.Precision.HIGHEST
LANES = 128
SUB = 8
F32 = jnp.float32
MESH = pl.DeviceIdType.MESH


def first_of(row):
    return SUB * (row // SUB)


def packed_outer(vectors):
    order = vectors.shape[0]
    return jnp.concatenate(
        [vectors[i : i + 1] * vectors[first_of(i) :] for i in range(order)], axis=0
    )


def damped_solve(packed, order):
    level = lax.broadcasted_iota(jnp.int32, (order, packed.shape[1]), 0)
    rows = []
    at = 0
    for i in range(order):
        low = first_of(i)
        rows.append(packed[at : at + order - low] + DAMP * (level[low:] == i).astype(F32))
        at += order - low
    remain = packed[at : at + order]
    inverse, forward = [], []
    for k in range(order):
        low = first_of(k)
        row = rows[k]
        inverse.append(1.0 / row[k - low : k - low + 1])
        scaled = row * inverse[k]
        for j in range(k + 1, order):
            begin = first_of(j)
            rows[j] = rows[j] - scaled[j - low : j - low + 1] * row[begin - low :]
        forward.append(remain[k : k + 1])
        part = remain[low:] - scaled * forward[k]
        remain = part if low == 0 else jnp.concatenate([remain[:low], part], axis=0)
    solved = jnp.zeros((order, packed.shape[1]), F32)
    for k in reversed(range(order)):
        low = first_of(k)
        known = jnp.sum(rows[k] * solved[low:], axis=0, keepdims=True)
        value = (forward[k] - known) * inverse[k]
        solved = jnp.where(level == k, value, solved)
    return solved


def spread_out(values, rows, cols):
    down, right = rows - values.shape[0], cols - values.shape[1]
    return jnp.pad(values, ((0, down), (0, right)))


def detrend_kernel(
    obj_n, ep_n, order, near, lc_ref, valid_ref, pixel_ref, sigma_ref, modes_ref,
    resid_ref, wq_ref, wb_ref,
    coef_s, modes_s, pix_send, pix_recv, ep_send, ep_recv, gram_send, gram_recv,
    mode_send, mode_recv, half_send, half_recv,
    pix_sem, ep_sem, gram_sem, mode_sem, half_sem,
):
    me_o, me_e = lax.axis_index("obj"), lax.axis_index("ep")
    rows, cols = lc_ref.shape
    blocks = cols // SUB
    share = rows // ep_n

    def device(do, de):
        return {
            "obj": lax.rem(me_o + do, obj_n),
            "ep": lax.rem(me_e + de, ep_n),
        }

    peers = list(near)
    peers += [(do, 0) for do in range(1, obj_n) if (do, 0) not in near]
    barrier = pltpu.get_barrier_semaphore()
    for do, de in peers:
        pl.semaphore_signal(barrier, inc=1, device_id=device(do, de), device_id_type=MESH)
    pl.semaphore_wait(barrier, len(peers))

    mask = valid_ref[...].astype(F32)
    sigma = sigma_ref[...]
    pixels = lax.broadcasted_iota(jnp.int32, (rows, pix_send.shape[2]), 1)
    member = (pixel_ref[...] == pixels).astype(F32)
    counts = jnp.sum(member * jnp.sum(mask, axis=1, keepdims=True), axis=0, keepdims=True)

    def residual():
        return lc_ref[...] - lax.dot_general(
            coef_s[...], modes_s[...], (((0,), (0,)), ((), ())),
            precision=HIGHEST, preferred_element_type=F32,
        )

    def robust(resid, phase):
        scaled = resid * sigma
        squares = jnp.sum(mask * scaled * scaled, axis=1, keepdims=True)
        sums = jnp.sum(member * squares, axis=0, keepdims=True)
        part = spread_out(jnp.concatenate([sums, counts], axis=0), SUB, sums.shape[1])
        pix_send[phase] = part
        copies = []
        for k, (do, de) in enumerate(near):
            copies.append(pltpu.make_async_remote_copy(
                src_ref=pix_send.at[phase], dst_ref=pix_recv.at[phase, k],
                send_sem=pix_sem.at[0, phase, k], recv_sem=pix_sem.at[1, phase, k],
                device_id=device(do, de), device_id_type=MESH,
            ))
            copies[k].start()
        for copy in copies:
            copy.wait()
        totals = part
        for k in range(len(near)):
            totals = totals + pix_recv[phase, k]
        spread = jnp.sqrt(totals[0:1] / jnp.maximum(totals[1:2], 1.0) + 1e-06)
        object_spread = jnp.sum(member * spread, axis=1, keepdims=True)
        zscore = scaled / object_spread
        huber = HUBER / jnp.maximum(jnp.abs(zscore), HUBER)
        return mask * huber * (sigma * sigma)

    coef_s[...] = jnp.zeros_like(coef_s)
    modes_s[...] = modes_ref[...]

    def iteration(it, carry):
        light = lc_ref[...]
        weight = robust(residual(), 2 * it)
        modes_t = modes_s[...]
        last = (((1,), (1,)), ((), ()))
        gram = lax.dot_general(
            packed_outer(modes_t), weight, last, precision=HIGHEST, preferred_element_type=F32
        )
        target = lax.dot_general(
            modes_t, weight * light, last, precision=HIGHEST, preferred_element_type=F32
        )
        packed = jnp.concatenate([gram, target], axis=0)
        ep_send[it] = packed
        copies = []
        for k in range(1, ep_n):
            copies.append(pltpu.make_async_remote_copy(
                src_ref=ep_send.at[it], dst_ref=ep_recv.at[it, k - 1],
                send_sem=ep_sem.at[0, it, k - 1], recv_sem=ep_sem.at[1, it, k - 1],
                device_id=device(0, k), device_id_type=MESH,
            ))
            copies[-1].start()
        for k in range(1, ep_n):
            copies[k - 1].wait()
            packed = packed + ep_recv[it, k - 1]
        coef_t = damped_solve(packed, order)
        coef_s[...] = coef_t

        weight = robust(residual(), 2 * it + 1)
        gram = jnp.dot(
            packed_outer(coef_t), weight, precision=HIGHEST, preferred_element_type=F32
        )
        target = jnp.dot(
            coef_t, weight * light, precision=HIGHEST, preferred_element_type=F32
        )
        packed = jnp.concatenate([gram, target], axis=0)
        depth = packed.shape[0]
        wide = gram_send.shape[3]
        turned = spread_out(packed, wide, cols).T
        gram_send[it] = turned.reshape(blocks, SUB, wide)
        copies = []
        for k in range(1, obj_n):
            there = lax.rem(me_o + k, obj_n)
            copies.append(pltpu.make_async_remote_copy(
                src_ref=gram_send.at[it, lax.rem(there, blocks)],
                dst_ref=gram_recv.at[it, k - 1],
                send_sem=gram_sem.at[0, it, k - 1], recv_sem=gram_sem.at[1, it, k - 1],
                device_id=device(k, 0), device_id_type=MESH,
            ))
            copies[-1].start()
        total = gram_send[it, lax.rem(me_o, blocks)]
        for k in range(1, obj_n):
            copies[k - 1].wait()
            total = total + gram_recv[it, k - 1]
        packed = spread_out(total, LANES, wide).T[:depth]
        solved = damped_solve(packed, order)
        mine = spread_out(solved, LANES, LANES).T[:SUB]
        mode_send[it] = mine
        mode_recv[it, me_o] = mine
        copies = []
        for k in range(1, obj_n):
            copies.append(pltpu.make_async_remote_copy(
                src_ref=mode_send.at[it], dst_ref=mode_recv.at[it, me_o],
                send_sem=mode_sem.at[0, it, k - 1], recv_sem=mode_sem.at[1, it, k - 1],
                device_id=device(k, 0), device_id_type=MESH,
            ))
            copies[-1].start()
        for copy in copies:
            copy.wait()
        modes_s[...] = mode_recv[it, :blocks].reshape(cols, LANES).T[:order]
        return carry

    lax.fori_loop(0, ITERS, iteration, 0)
    resid = residual()
    resid_ref[...] = resid
    weight = robust(resid, 2 * ITERS)
    half_send[0] = (weight * resid).astype(jnp.bfloat16)
    half_send[1] = weight.astype(jnp.bfloat16)
    copies = []
    for k in range(1, ep_n):
        there = lax.rem(me_e + k, ep_n)
        copies.append(pltpu.make_async_remote_copy(
            src_ref=half_send.at[:, pl.ds(pl.multiple_of(there * share, share), share), :],
            dst_ref=half_recv.at[me_e],
            send_sem=half_sem.at[0, k - 1], recv_sem=half_sem.at[1, k - 1],
            device_id=device(0, k), device_id_type=MESH,
        ))
        copies[-1].start()
    half_recv[me_e] = half_send[:, pl.ds(pl.multiple_of(me_e * share, share), share), :]
    for copy in copies:
        copy.wait()
    for e in range(ep_n):
        wq_ref[:, e * cols : (e + 1) * cols] = half_recv[e, 0]
        wb_ref[:, e * cols : (e + 1) * cols] = half_recv[e, 1]


SIN_TERMS = [(-1.0) ** n / math.factorial(2 * n + 1) for n in range(7)]
COS_TERMS = [(-1.0) ** n / math.factorial(2 * n) for n in range(8)]


def series(square, terms):
    value = jnp.full_like(square, terms[-1])
    for term in terms[-2::-1]:
        value = value * square + term
    return value


def power_kernel(wq_ref, wb_ref, times_ref, freqs_ref, power_ref):
    values, weights = wq_ref[...], wb_ref[...]
    total = jnp.sum(weights.astype(F32), axis=1, keepdims=True)
    level = jnp.sum(values.astype(F32), axis=1, keepdims=True)
    cycles = times_ref[...] * freqs_ref[...]
    cycles = cycles - jnp.floor(cycles)
    turn = jnp.where(cycles >= 0.5, cycles - 1.0, cycles)
    angle = (2.0 * math.pi) * (jnp.abs(turn) - 0.25)
    square = angle * angle
    cos_b = -angle * series(square, SIN_TERMS)
    size = series(square, COS_TERMS)
    sin_b = jnp.where(turn < 0.0, -size, size)

    def sums(rows, basis):
        return jnp.dot(rows, basis.astype(jnp.bfloat16), preferred_element_type=F32)

    both = jnp.concatenate([weights, values], axis=0)
    count = weights.shape[0]
    by_cos = sums(both, cos_b)
    by_sin = sums(both, sin_b)
    cosine, sine = by_cos[:count], by_sin[:count]
    cosine_two = sums(weights, 2.0 * cos_b * cos_b - 1.0)
    sine_two = sums(weights, 2.0 * sin_b * cos_b)
    inverse = 1.0 / total
    mean_level = level * inverse
    ycos = by_cos[count:] - mean_level * cosine
    ysin = by_sin[count:] - mean_level * sine
    cc_term = 0.5 * (total + cosine_two) - cosine * cosine * inverse + RIDGE * total
    ss_term = 0.5 * (total - cosine_two) - sine * sine * inverse + RIDGE * total
    cs_term = 0.5 * sine_two - cosine * sine * inverse
    determinant = cc_term * ss_term - cs_term * cs_term
    power_ref[...] = (
        ss_term * ycos * ycos + cc_term * ysin * ysin - 2.0 * cs_term * ycos * ysin
    ) / determinant


def per_device(light_curves, valid, pixel, inv_sigma, modes_init, epoch_jitter, freq_index):
    obj_n = lax.axis_size("obj")
    ep_n = lax.axis_size("ep")
    order = modes_init.shape[1]
    rows, cols = light_curves.shape
    share = rows // ep_n
    epochs = epoch_jitter.shape[0]
    pix_lanes = -(-4 * obj_n // LANES) * LANES
    near = [
        (do, de)
        for do in sorted({0, 1 % obj_n, (obj_n - 1) % obj_n})
        for de in range(ep_n)
        if (do, de) != (0, 0)
    ]
    depth = sum(order - first_of(i) for i in range(order)) + order
    wide = -(-depth // LANES) * LANES
    phases = 2 * ITERS + 1
    vmem = pl.BlockSpec(memory_space=pltpu.VMEM)
    sem = pltpu.SemaphoreType.DMA
    residual, values, weights = pl.pallas_call(
        functools.partial(detrend_kernel, obj_n, ep_n, order, near),
        out_shape=(
            jax.ShapeDtypeStruct((rows, cols), F32),
            jax.ShapeDtypeStruct((share, epochs), jnp.bfloat16),
            jax.ShapeDtypeStruct((share, epochs), jnp.bfloat16),
        ),
        in_specs=[vmem] * 5,
        out_specs=(vmem,) * 3,
        scratch_shapes=[
            pltpu.VMEM((order, rows), F32),
            pltpu.VMEM((order, cols), F32),
            pltpu.VMEM((phases, SUB, pix_lanes), F32),
            pltpu.VMEM((phases, len(near), SUB, pix_lanes), F32),
            pltpu.VMEM((ITERS, depth, rows), F32),
            pltpu.VMEM((ITERS, max(ep_n - 1, 1), depth, rows), F32),
            pltpu.VMEM((ITERS, cols // SUB, SUB, wide), F32),
            pltpu.VMEM((ITERS, max(obj_n - 1, 1), SUB, wide), F32),
            pltpu.VMEM((ITERS, SUB, LANES), F32),
            pltpu.VMEM((ITERS, max(obj_n, cols // SUB), SUB, LANES), F32),
            pltpu.VMEM((2, rows, cols), jnp.bfloat16),
            pltpu.VMEM((ep_n, 2, share, cols), jnp.bfloat16),
            sem((2, phases, len(near))),
            sem((2, ITERS, max(ep_n - 1, 1))),
            sem((2, ITERS, max(obj_n - 1, 1))),
            sem((2, ITERS, max(obj_n - 1, 1))),
            sem((2, max(ep_n - 1, 1))),
        ],
        compiler_params=pltpu.CompilerParams(collective_id=0, has_side_effects=True),
    )(light_curves, valid, pixel[:, None], inv_sigma[:, None], modes_init.T)

    times = jnp.arange(epochs, dtype=jnp.int32).astype(F32) + epoch_jitter
    freqs = (freq_index + 1).astype(F32) / (4.0 * epochs)
    count = freqs.shape[0]
    size = math.gcd(count, 256)
    whole = lambda shape: pl.BlockSpec(shape, lambda i: (0, 0))
    power = pl.pallas_call(
        power_kernel,
        grid=(count // size,),
        out_shape=jax.ShapeDtypeStruct((share, count), F32),
        in_specs=[
            whole((share, epochs)),
            whole((share, epochs)),
            whole((epochs, 1)),
            pl.BlockSpec((1, size), lambda i: (0, i)),
        ],
        out_specs=pl.BlockSpec((share, size), lambda i: (0, i)),
    )(values, weights, times[:, None], freqs[None, :])
    return (residual, power)


def solution(mesh):
    in_specs = (P("obj", "ep"), P("obj", "ep"), P("obj"), P("obj"), P("ep", None), P(), P())
    out_specs = (P("obj", "ep"), P(("obj", "ep"), None))
    return jax.shard_map(
        per_device, mesh=mesh, in_specs=in_specs, out_specs=out_specs, check_vma=False
    )
```

time: 402 us -> 74.2 us (0.18); the launches traced: 395 us -> 73.9 us
  waiting for transfers between devices: 156 us -> 0 us
  blocking collectives: 104 us -> 0 us
  Pallas kernels: 0 us -> 68.4 us
  other arithmetic: 68.2 us -> 1.29 us
  starting transfers between devices: 28.2 us -> 0 us
  between operations: 16.6 us -> 0.65 us
  matrix products: 9.14 us -> 0 us
  local copies, waits for them, and re-layouts: 12.2 us -> 3.57 us
    psum x4 -> x0, waiting for transfers between devices: 150 us -> none  [the longest x2 111 us: per_device(): gram, target = lax.psum((gram, target), 'obj')]
    psum x9 -> x0, blocking collectives: 104 us -> none  [the longest x2 68.6 us: per_device(): gram, target = lax.psum((gram, target), 'obj')]
    pallas_call x0 -> x2, Pallas kernels: none -> 68.4 us  [the longest x1 61.2 us: per_device(): pl.pallas_call(functools.partial(detrend_kernel, obj_n, ep_n, order, near...]
    ppermute x10 -> x0, starting transfers between devices: 21.6 us -> none  [the longest x5 15.2 us: with_halo(): lax.ppermute(tail, axis, [(i, (i + 1) % count) for i in range(ends)])]
    another operation x23 -> x0, other arithmetic: 18.1 us -> none
    sub x115 -> x0, other arithmetic: 16.2 us -> none  [the longest x60 10 us: damped_solve(): column = column - jnp.sum(earlier * earlier[column_at][None], axis=1)]
    unnamed x56 -> x0, other arithmetic: 12.5 us -> none
    dot_general x31 -> x0, matrix products: 9.14 us -> none  [the longest x4 1.87 us: spectrum_sums(): jnp.dot(weighted, basis[:, :2 * width], preferred_element_type=jnp.float32)]
  transfers between devices with their start and end apart: 16 -> 0, of which waited for: 9 -> 0; matrix products, arithmetic and copies ran while one was open for 5% -> 0% of each run, Pallas kernels for 0% -> 0%
where the time goes in v1:
time: 74.2 us; the launch traced here: 73.9 us
  Pallas kernels  68.4 us (92%)
  local copies, waits for them, and re-layouts  3.57 us (5%)
  other arithmetic  1.29 us (2%)
    pallas_call x1, Pallas kernels, per_device(): pl.pallas_call(functools.partial(detrend_kernel, obj_n, ep_n, order, near...  61.2 us
    pallas_call x1, Pallas kernels, per_device(): pl.pallas_call(power_kernel, grid=(count // size,), out_shape=jax.ShapeDt...  7.14 us

profile of v1, /device:TPU:0, one launch (start us, length us, event | category | flops | bytes accessed | tf_op | source)
XLA Modules:
  0.0 73.9 jit_solution(16244693842090283888)
XLA Ops:
  0.6 0.0 copy-start.1
  0.6 0.7 convert_add_fusion
  1.3 0.0 copy-done.1
  1.3 0.6 convert_multiply_fusion
  1.9 0.0 copy-start.2
  1.9 0.7 copy-done.2
  2.6 0.0 copy-start.3
  2.6 0.7 %copy.11.pixel_ref = s32[128,1]{1,0:T(8,128)} copy(s32[128,1]{0,1:T(1,128)S(1)} %bitcast.8) | data formatting | bytes 1024 | tf_op jit(solution)/shard_map/broadcast_in_dim | solution.py:325
  3.3 0.0 copy-done.3
  3.3 0.7 %copy.12.sigma_ref = f32[128,1]{1,0:T(8,128)} copy(f32[128,1]{0,1:T(1,128)S(1)} %bitcast.9) | data formatting | bytes 1024 | tf_op jit(solution)/shard_map/broadcast_in_dim | solution.py:325
  4.1 61.2 %shard_map.86 = (f32[128,128]{1,0:T(8,128)}, bf16[64,256]{1,0:T(8,128)(2,1)}, bf16[64,256]{1,0:T(8,128)(2,1)}) custom-call(f32[128,128]{1,0:T(8,128)} %lc_ref.1, s32[128,128]{1,0:T(8,128)} %valid_ref.1, s32[128,1]{1,0:T(8,128)} %copy.11.pixel_ref, f32[128,1]{1,0:T(8,128)} %copy.12.sigma_ref, f32[16,128]{1,0:T(8,128)} %bitcast.6), custom_call_target="tpu_custom_call" | custom-call | tf_op jit(solution)/shard_map/pallas_call | solution.py:296
  65.3 0.8 %copy.13.times_ref = f32[256,1]{1,0:T(8,128)} copy(f32[256,1]{0,1:T(1,128)S(1)} %bitcast.7) | data formatting | bytes 2048 | tf_op jit(solution)/shard_map/broadcast_in_dim | solution.py:343
  66.1 0.0 copy-start
  66.1 7.1 %shard_map.87 = f32[64,2048]{1,0:T(8,128)} custom-call(bf16[64,256]{1,0:T(8,128)(2,1)} %get-tuple-element.6.wq_ref, bf16[64,256]{1,0:T(8,128)(2,1)} %get-tuple-element.7.wb_ref, f32[256,1]{1,0:T(8,128)} %copy.13.times_ref, f32[1,2048]{1,0:T(1,128)} %bitcast.5), custom_call_target="tpu_custom_call" | custom-call | tf_op jit(solution)/shard_map/pallas_call | solution.py:332
  73.3 0.0 copy-done
  73.3 0.6 copy.15
Async XLA Ops:
  0.6 0.7 copy-start.1
  1.9 0.7 copy-start.2
  2.6 0.7 %copy-start.3 = (f32[128]{0:T(128)S(1)}, f32[128]{0:T(128)}, u32[]{:S(2)}) copy-start(f32[128]{0:T(128)} %param.10) | copy-start | bytes 1540
  66.1 7.1 %copy-start = (f32[128,128]{1,0:T(8,128)S(1)}, f32[128,128]{1,0:T(8,128)}, u32[]{:S(2)}) copy-start(f32[128,128]{1,0:T(8,128)} %get-tuple-element.10) | copy-start | bytes 196612

commit v2 on v1

--- a/solution.py
+++ b/solution.py
@@ -18,6 +18,7 @@
 LANES = 128
 SUB = 8
 F32 = jnp.float32
+STRIP = 32
 MESH = pl.DeviceIdType.MESH
 
 
@@ -67,9 +68,13 @@
     return jnp.pad(values, ((0, down), (0, right)))
 
 
+def as_column(row):
+    return jnp.broadcast_to(row, (LANES, row.shape[1])).T
+
+
 def detrend_kernel(
     obj_n, ep_n, order, near, lc_ref, valid_ref, pixel_ref, sigma_ref, modes_ref,
-    resid_ref, wq_ref, wb_ref,
+    jitter_ref, freq_ref, resid_ref, power_ref, basis_s, times_s,
     coef_s, modes_s, pix_send, pix_recv, ep_send, ep_recv, gram_send, gram_recv,
     mode_send, mode_recv, half_send, half_recv,
     pix_sem, ep_sem, gram_sem, mode_sem, half_sem,
@@ -93,9 +98,28 @@
     pl.semaphore_wait(barrier, len(peers))
 
     mask = valid_ref[...].astype(F32)
-    sigma = sigma_ref[...]
+    sigma = as_column(sigma_ref[...])[:, :1]
+    epochs = jitter_ref.shape[1]
+    times_s[...] = as_column(
+        lax.broadcasted_iota(jnp.int32, (1, epochs), 1).astype(F32) + jitter_ref[...]
+    )
+    width = basis_s.shape[3]
+
+    def fill_basis(block):
+        begin = pl.multiple_of(block * width, width)
+        freqs = (freq_ref[:, pl.ds(begin, width)] + 1).astype(F32) / (4.0 * epochs)
+
+        def strip(step, carry):
+            at = pl.ds(pl.multiple_of(step * STRIP, STRIP), STRIP)
+            times = jnp.concatenate([times_s[at, :]] * (width // LANES), axis=1)
+            for kind, values in enumerate(basis_of(times * freqs)):
+                basis_s[block, kind, at, :] = values.astype(jnp.bfloat16)
+            return carry
+
+        lax.fori_loop(0, epochs // STRIP, strip, 0)
+
     pixels = lax.broadcasted_iota(jnp.int32, (rows, pix_send.shape[2]), 1)
-    member = (pixel_ref[...] == pixels).astype(F32)
+    member = (as_column(pixel_ref[...].astype(F32))[:, :1] == pixels.astype(F32)).astype(F32)
     counts = jnp.sum(member * jnp.sum(mask, axis=1, keepdims=True), axis=0, keepdims=True)
 
     def residual():
@@ -104,7 +128,7 @@
             precision=HIGHEST, preferred_element_type=F32,
         )
 
-    def robust(resid, phase):
+    def robust(resid, phase, block=None):
         scaled = resid * sigma
         squares = jnp.sum(mask * scaled * scaled, axis=1, keepdims=True)
         sums = jnp.sum(member * squares, axis=0, keepdims=True)
@@ -118,6 +142,8 @@
                 device_id=device(do, de), device_id_type=MESH,
             ))
             copies[k].start()
+        if block is not None:
+            fill_basis(block)
         for copy in copies:
             copy.wait()
         totals = part
@@ -130,11 +156,11 @@
         return mask * huber * (sigma * sigma)
 
     coef_s[...] = jnp.zeros_like(coef_s)
-    modes_s[...] = modes_ref[...]
+    modes_s[...] = spread_out(modes_ref[...], cols, LANES).T[:order]
 
     def iteration(it, carry):
         light = lc_ref[...]
-        weight = robust(residual(), 2 * it)
+        weight = robust(residual(), 2 * it, 4 * it)
         modes_t = modes_s[...]
         last = (((1,), (1,)), ((), ()))
         gram = lax.dot_general(
@@ -159,7 +185,7 @@
         coef_t = damped_solve(packed, order)
         coef_s[...] = coef_t
 
-        weight = robust(residual(), 2 * it + 1)
+        weight = robust(residual(), 2 * it + 1, 4 * it + 1)
         gram = jnp.dot(
             packed_outer(coef_t), weight, precision=HIGHEST, preferred_element_type=F32
         )
@@ -181,6 +207,7 @@
                 device_id=device(k, 0), device_id_type=MESH,
             ))
             copies[-1].start()
+        fill_basis(4 * it + 2)
         total = gram_send[it, lax.rem(me_o, blocks)]
         for k in range(1, obj_n):
             copies[k - 1].wait()
@@ -198,6 +225,7 @@
                 device_id=device(k, 0), device_id_type=MESH,
             ))
             copies[-1].start()
+        fill_basis(4 * it + 3)
         for copy in copies:
             copy.wait()
         modes_s[...] = mode_recv[it, :blocks].reshape(cols, LANES).T[:order]
@@ -222,9 +250,26 @@
     half_recv[me_e] = half_send[:, pl.ds(pl.multiple_of(me_e * share, share), share), :]
     for copy in copies:
         copy.wait()
-    for e in range(ep_n):
-        wq_ref[:, e * cols : (e + 1) * cols] = half_recv[e, 0]
-        wb_ref[:, e * cols : (e + 1) * cols] = half_recv[e, 1]
+    received = [half_recv[e] for e in range(ep_n)]
+    values = jnp.concatenate([half[0] for half in received], axis=1)
+    weights = jnp.concatenate([half[1] for half in received], axis=1)
+    both = jnp.concatenate([weights, values], axis=0)
+    total = jnp.sum(weights.astype(F32), axis=1, keepdims=True)
+    level = jnp.sum(values.astype(F32), axis=1, keepdims=True)
+
+    def spectrum(block, carry):
+        at = pl.ds(pl.multiple_of(block * width, width), width)
+        power_ref[:, at] = powers(
+            jnp.dot(both, basis_s[block, 0], preferred_element_type=F32),
+            jnp.dot(both, basis_s[block, 1], preferred_element_type=F32),
+            jnp.dot(weights, basis_s[block, 2], preferred_element_type=F32),
+            jnp.dot(weights, basis_s[block, 3], preferred_element_type=F32),
+            total,
+            level,
+        )
+        return carry
+
+    lax.fori_loop(0, basis_s.shape[0], spectrum, 0)
 
 
 SIN_TERMS = [(-1.0) ** n / math.factorial(2 * n + 1) for n in range(7)]
@@ -238,29 +283,20 @@
     return value
 
 
-def power_kernel(wq_ref, wb_ref, times_ref, freqs_ref, power_ref):
-    values, weights = wq_ref[...], wb_ref[...]
-    total = jnp.sum(weights.astype(F32), axis=1, keepdims=True)
-    level = jnp.sum(values.astype(F32), axis=1, keepdims=True)
-    cycles = times_ref[...] * freqs_ref[...]
+def basis_of(cycles):
     cycles = cycles - jnp.floor(cycles)
     turn = jnp.where(cycles >= 0.5, cycles - 1.0, cycles)
     angle = (2.0 * math.pi) * (jnp.abs(turn) - 0.25)
     square = angle * angle
-    cos_b = -angle * series(square, SIN_TERMS)
+    cosine = -angle * series(square, SIN_TERMS)
     size = series(square, COS_TERMS)
-    sin_b = jnp.where(turn < 0.0, -size, size)
-
-    def sums(rows, basis):
-        return jnp.dot(rows, basis.astype(jnp.bfloat16), preferred_element_type=F32)
-
-    both = jnp.concatenate([weights, values], axis=0)
-    count = weights.shape[0]
-    by_cos = sums(both, cos_b)
-    by_sin = sums(both, sin_b)
+    sine = jnp.where(turn < 0.0, -size, size)
+    return cosine, sine, 2.0 * cosine * cosine - 1.0, 2.0 * sine * cosine
+
+
+def powers(by_cos, by_sin, cosine_two, sine_two, total, level):
+    count = cosine_two.shape[0]
     cosine, sine = by_cos[:count], by_sin[:count]
-    cosine_two = sums(weights, 2.0 * cos_b * cos_b - 1.0)
-    sine_two = sums(weights, 2.0 * sin_b * cos_b)
     inverse = 1.0 / total
     mean_level = level * inverse
     ycos = by_cos[count:] - mean_level * cosine
@@ -269,7 +305,7 @@
     ss_term = 0.5 * (total - cosine_two) - sine * sine * inverse + RIDGE * total
     cs_term = 0.5 * sine_two - cosine * sine * inverse
     determinant = cc_term * ss_term - cs_term * cs_term
-    power_ref[...] = (
+    return (
         ss_term * ycos * ycos + cc_term * ysin * ysin - 2.0 * cs_term * ycos * ysin
     ) / determinant
 
@@ -293,16 +329,19 @@
     phases = 2 * ITERS + 1
     vmem = pl.BlockSpec(memory_space=pltpu.VMEM)
     sem = pltpu.SemaphoreType.DMA
-    residual, values, weights = pl.pallas_call(
+    count = freq_index.shape[0]
+    parts = 4 * ITERS
+    return pl.pallas_call(
         functools.partial(detrend_kernel, obj_n, ep_n, order, near),
         out_shape=(
             jax.ShapeDtypeStruct((rows, cols), F32),
-            jax.ShapeDtypeStruct((share, epochs), jnp.bfloat16),
-            jax.ShapeDtypeStruct((share, epochs), jnp.bfloat16),
+            jax.ShapeDtypeStruct((share, count), F32),
         ),
-        in_specs=[vmem] * 5,
-        out_specs=(vmem,) * 3,
+        in_specs=[vmem] * 7,
+        out_specs=(vmem,) * 2,
         scratch_shapes=[
+            pltpu.VMEM((parts, 4, epochs, count // parts), jnp.bfloat16),
+            pltpu.VMEM((epochs, LANES), F32),
             pltpu.VMEM((order, rows), F32),
             pltpu.VMEM((order, cols), F32),
             pltpu.VMEM((phases, SUB, pix_lanes), F32),
@@ -322,26 +361,10 @@
             sem((2, max(ep_n - 1, 1))),
         ],
         compiler_params=pltpu.CompilerParams(collective_id=0, has_side_effects=True),
-    )(light_curves, valid, pixel[:, None], inv_sigma[:, None], modes_init.T)
-
-    times = jnp.arange(epochs, dtype=jnp.int32).astype(F32) + epoch_jitter
-    freqs = (freq_index + 1).astype(F32) / (4.0 * epochs)
-    count = freqs.shape[0]
-    size = math.gcd(count, 256)
-    whole = lambda shape: pl.BlockSpec(shape, lambda i: (0, 0))
-    power = pl.pallas_call(
-        power_kernel,
-        grid=(count // size,),
-        out_shape=jax.ShapeDtypeStruct((share, count), F32),
-        in_specs=[
-            whole((share, epochs)),
-            whole((share, epochs)),
-            whole((epochs, 1)),
-            pl.BlockSpec((1, size), lambda i: (0, i)),
-        ],
-        out_specs=pl.BlockSpec((share, size), lambda i: (0, i)),
-    )(values, weights, times[:, None], freqs[None, :])
-    return (residual, power)
+    )(
+        light_curves, valid, pixel[None], inv_sigma[None], modes_init,
+        epoch_jitter[None], freq_index[None],
+    )
 
 
 def solution(mesh):

time: 74.2 us -> 69.4 us (0.935)
  Pallas kernels: 68.4 us -> 63.7 us
  other arithmetic: 1.29 us -> 0 us
  local copies, waits for them, and re-layouts: 3.57 us -> 4.77 us
    pallas_call x1 -> x0, Pallas kernels: 7.14 us -> none  [per_device(): pl.pallas_call(power_kernel, grid=(count // size,), out_shape=jax.ShapeDt...]
    unnamed x9 -> x3, local copies, waits for them, and re-layouts: 1.3 us -> 4.77 us
    pallas_call x1, Pallas kernels: 61.2 us -> 63.7 us  [per_device(): pl.pallas_call(functools.partial(detrend_kernel, obj_n, ep_n, order, near...]
    broadcast_in_dim x3 -> x0, local copies, waits for them, and re-layouts: 2.28 us -> none  [the longest x1 0.8 us: per_device(): times[:, None]]
where the time goes in v2:
time: 69.4 us; the launch traced here: 69.1 us
  Pallas kernels  63.7 us (92%)
  local copies, waits for them, and re-layouts  4.77 us (7%)
    pallas_call x1, Pallas kernels, per_device(): pl.pallas_call(functools.partial(detrend_kernel, obj_n, ep_n, order, near...  63.7 us
    unnamed x3, local copies, waits for them, and re-layouts  4.77 us

profile of v2, /device:TPU:0, one launch (start us, length us, event | category | flops | bytes accessed | tf_op | source)
XLA Modules:
  0.0 69.1 jit_solution(1620486477453626263)
XLA Ops:
  0.6 1.4 %copy.9.modes_ref = f32[128,16]{1,0:T(8,128)} copy(f32[128,16]{0,1:T(8,128)} %param.11) | data formatting | bytes 16384 | tf_op args[4]
  2.1 63.7 %shard_map.86 = (f32[128,128]{1,0:T(8,128)}, f32[64,2048]{1,0:T(8,128)}) custom-call(f32[128,128]{1,0:T(8,128)} %lc_ref.1, s32[128,128]{1,0:T(8,128)} %valid_ref.1, s32[1,128]{1,0:T(1,128)} %bitcast.6, f32[1,128]{1,0:T(1,128)} %bitcast.7, f32[128,16]{1,0:T(8,128)} %copy.9.modes_ref, f32[1,256]{1,0:T(1,128)} %bitcast.5, s32[1,2048]{1,0:T(1,128)} %bitcast.4), custom_call_target="tpu_custom_call" | custom-call | tf_op jit(solution)/shard_map/pallas_call | solution.py:334
  65.8 1.5 %copy.12 = f32[128,128]{1,0:T(8,128)} copy(f32[128,128]{1,0:T(8,128)} %get-tuple-element.4) | data formatting | bytes 131072
  67.3 1.9 %copy.13 = f32[64,2048]{1,0:T(8,128)} copy(f32[64,2048]{1,0:T(8,128)} %get-tuple-element.5) | data formatting | bytes 1048576

commit v3 on v2

--- a/solution.py
+++ b/solution.py
@@ -97,6 +97,24 @@
         pl.semaphore_signal(barrier, inc=1, device_id=device(do, de), device_id_type=MESH)
     pl.semaphore_wait(barrier, len(peers))
 
+    def sends_to(do):
+        return None if do == 0 else me_o < obj_n - 1 if do == 1 else me_o > 0
+
+    def hears_from(do):
+        return None if do == 0 else me_o > 0 if do == 1 else me_o < obj_n - 1
+
+    def guarded(condition, action):
+        if condition is None:
+            action()
+        else:
+            pl.when(condition)(action)
+
+    for k, (do, de) in enumerate(near):
+        if do != 0:
+            @pl.when(jnp.logical_not(hears_from(do)))
+            def _():
+                pix_recv[:, k] = jnp.zeros(pix_recv.shape[:1] + pix_recv.shape[2:], F32)
+
     mask = valid_ref[...].astype(F32)
     sigma = as_column(sigma_ref[...])[:, :1]
     epochs = jitter_ref.shape[1]
@@ -141,11 +159,12 @@
                 send_sem=pix_sem.at[0, phase, k], recv_sem=pix_sem.at[1, phase, k],
                 device_id=device(do, de), device_id_type=MESH,
             ))
-            copies[k].start()
+            guarded(sends_to(do), copies[k].start)
         if block is not None:
             fill_basis(block)
-        for copy in copies:
-            copy.wait()
+        for k, (do, de) in enumerate(near):
+            guarded(sends_to(do), copies[k].wait_send)
+            guarded(hears_from(do), copies[k].wait_recv)
         totals = part
         for k in range(len(near)):
             totals = totals + pix_recv[phase, k]
@@ -156,7 +175,7 @@
         return mask * huber * (sigma * sigma)
 
     coef_s[...] = jnp.zeros_like(coef_s)
-    modes_s[...] = spread_out(modes_ref[...], cols, LANES).T[:order]
+    modes_s[...] = modes_ref[...]
 
     def iteration(it, carry):
         light = lc_ref[...]
@@ -320,8 +339,8 @@
     pix_lanes = -(-4 * obj_n // LANES) * LANES
     near = [
         (do, de)
-        for do in sorted({0, 1 % obj_n, (obj_n - 1) % obj_n})
-        for de in range(ep_n)
+        for do in sorted({0, 1 % obj_n, (obj_n - 1) % obj_n}, reverse=True)
+        for de in reversed(range(ep_n))
         if (do, de) != (0, 0)
     ]
     depth = sum(order - first_of(i) for i in range(order)) + order
@@ -362,7 +381,7 @@
         ],
         compiler_params=pltpu.CompilerParams(collective_id=0, has_side_effects=True),
     )(
-        light_curves, valid, pixel[None], inv_sigma[None], modes_init,
+        light_curves, valid, pixel[None], inv_sigma[None], modes_init.T,
         epoch_jitter[None], freq_index[None],
     )
 

time: 69.4 us -> 66.4 us (0.957)
  Pallas kernels: 63.7 us -> 62.1 us
  local copies, waits for them, and re-layouts: 4.77 us -> 3.34 us
    pallas_call x1, Pallas kernels: 63.7 us -> 62.1 us  [per_device(): pl.pallas_call(functools.partial(detrend_kernel, obj_n, ep_n, order, near...]
    unnamed x3 -> x2, local copies, waits for them, and re-layouts: 4.77 us -> 3.34 us
where the time goes in v3:
time: 66.4 us; the launch traced here: 66.1 us
  Pallas kernels  62.1 us (94%)
  local copies, waits for them, and re-layouts  3.34 us (5%)
    pallas_call x1, Pallas kernels, per_device(): pl.pallas_call(functools.partial(detrend_kernel, obj_n, ep_n, order, near...  62.1 us
    unnamed x2, local copies, waits for them, and re-layouts  3.34 us

profile of v3, /device:TPU:0, one launch (start us, length us, event | category | flops | bytes accessed | tf_op | source)
XLA Modules:
  0.0 66.1 jit_solution(1653840756131972785)
XLA Ops:
  0.6 62.1 %shard_map.86 = (f32[128,128]{1,0:T(8,128)}, f32[64,2048]{1,0:T(8,128)}) custom-call(f32[128,128]{1,0:T(8,128)} %lc_ref.1, s32[128,128]{1,0:T(8,128)} %valid_ref.1, s32[1,128]{1,0:T(1,128)} %bitcast.8, f32[1,128]{1,0:T(1,128)} %bitcast.9, f32[16,128]{1,0:T(8,128)} %bitcast.5, f32[1,256]{1,0:T(1,128)} %bitcast.7, s32[1,2048]{1,0:T(1,128)} %bitcast.6), custom_call_target="tpu_custom_call" | custom-call | tf_op jit(solution)/shard_map/pallas_call | solution.py:353
  62.8 1.5 %copy.11 = f32[128,128]{1,0:T(8,128)} copy(f32[128,128]{1,0:T(8,128)} %get-tuple-element.4) | data formatting | bytes 131072
  64.3 1.9 %copy.12 = f32[64,2048]{1,0:T(8,128)} copy(f32[64,2048]{1,0:T(8,128)} %get-tuple-element.5) | data formatting | bytes 1048576

commit v4 on v3

--- a/solution.py
+++ b/solution.py
@@ -82,6 +82,7 @@
     me_o, me_e = lax.axis_index("obj"), lax.axis_index("ep")
     rows, cols = lc_ref.shape
     blocks = cols // SUB
+    far = sorted(range(1, obj_n), key=lambda k: abs(2 * k - obj_n))
     share = rows // ep_n
 
     def device(do, de):
@@ -217,7 +218,7 @@
         turned = spread_out(packed, wide, cols).T
         gram_send[it] = turned.reshape(blocks, SUB, wide)
         copies = []
-        for k in range(1, obj_n):
+        for k in far:
             there = lax.rem(me_o + k, obj_n)
             copies.append(pltpu.make_async_remote_copy(
                 src_ref=gram_send.at[it, lax.rem(there, blocks)],
@@ -228,8 +229,8 @@
             copies[-1].start()
         fill_basis(4 * it + 2)
         total = gram_send[it, lax.rem(me_o, blocks)]
-        for k in range(1, obj_n):
-            copies[k - 1].wait()
+        for k, copy in zip(far, copies):
+            copy.wait()
             total = total + gram_recv[it, k - 1]
         packed = spread_out(total, LANES, wide).T[:depth]
         solved = damped_solve(packed, order)
@@ -237,7 +238,7 @@
         mode_send[it] = mine
         mode_recv[it, me_o] = mine
         copies = []
-        for k in range(1, obj_n):
+        for k in far:
             copies.append(pltpu.make_async_remote_copy(
                 src_ref=mode_send.at[it], dst_ref=mode_recv.at[it, me_o],
                 send_sem=mode_sem.at[0, it, k - 1], recv_sem=mode_sem.at[1, it, k - 1],

time: 66.4 us -> 66.4 us (level)
  no operation moved by 1% of the time
where the time goes in v4:
time: 66.4 us; the launch traced here: 66.2 us
  Pallas kernels  62.2 us (94%)
  local copies, waits for them, and re-layouts  3.34 us (5%)
    pallas_call x1, Pallas kernels, per_device(): pl.pallas_call(functools.partial(detrend_kernel, obj_n, ep_n, order, near...  62.2 us
    unnamed x2, local copies, waits for them, and re-layouts  3.34 us

profile of v4, /device:TPU:0, one launch (start us, length us, event | category | flops | bytes accessed | tf_op | source)
XLA Modules:
  0.0 66.2 jit_solution(12859763995386545159)
XLA Ops:
  0.6 62.2 %shard_map.86 = (f32[128,128]{1,0:T(8,128)}, f32[64,2048]{1,0:T(8,128)}) custom-call(f32[128,128]{1,0:T(8,128)} %lc_ref.1, s32[128,128]{1,0:T(8,128)} %valid_ref.1, s32[1,128]{1,0:T(1,128)} %bitcast.8, f32[1,128]{1,0:T(1,128)} %bitcast.9, f32[16,128]{1,0:T(8,128)} %bitcast.5, f32[1,256]{1,0:T(1,128)} %bitcast.7, s32[1,2048]{1,0:T(1,128)} %bitcast.6), custom_call_target="tpu_custom_call" | custom-call | tf_op jit(solution)/shard_map/pallas_call | solution.py:354
  62.8 1.5 %copy.11 = f32[128,128]{1,0:T(8,128)} copy(f32[128,128]{1,0:T(8,128)} %get-tuple-element.4) | data formatting | bytes 131072
  64.3 1.9 %copy.12 = f32[64,2048]{1,0:T(8,128)} copy(f32[64,2048]{1,0:T(8,128)} %get-tuple-element.5) | data formatting | bytes 1048576
